TPU v7x, 32 devices: a whole 2x2x4 slice. The times are simulated.
32 devices in a mesh: dp: 8 (over z, x), sp: 4 (over y, core).
Axes of the slice: x: 2, y: 2, z: 4, core: 2. Of those that a mesh axis runs over, the one named last changes fastest.
Arguments:
- tokens: bfloat16 [8192, 768], P(('dp', 'sp')), may hold values from -6 to 6
- segment_ids: int32 [8, 1024], P('dp'), may hold values from 0 to 3, never falling along the last dimension, each value on 1 to 512 neighbouring positions
- masked_rows: int32 [2432], P(('dp', 'sp')), may hold values from 0 to 255, as said below
- replacement: bfloat16 [2432, 768], P(('dp', 'sp')), may hold values from -6 to 6
- cotangent: float32 [2432, 768], P(('dp', 'sp')), may hold values from -6 to 6
- w_qkv: bfloat16 [768, 2304], replicated, may hold values from -0.21875 to 0.21875
- w_out_attn: bfloat16 [768, 768], replicated, may hold values from -0.875 to 0.875
- w_in_ff: bfloat16 [768, 6144], replicated, may hold values from -0.21875 to 0.21875
- w_out_ff: bfloat16 [3072, 768], replicated, may hold values from -0.109375 to 0.109375
- gain_one: float32 [768], replicated, may hold values from 0.1 to 1.9
- shift_one: float32 [768], replicated, may hold values from -3 to 3
- gain_two: float32 [768], replicated, may hold values from 0.1 to 1.9
- shift_two: float32 [768], replicated, may hold values from -3 to 3
Outputs:
- layer_out: bfloat16 [8192, 768], P(('dp', 'sp'))
- grad_tokens: float32 [8192, 768], P(('dp', 'sp'))
- grad_replacement: float32 [2432, 768], P(('dp', 'sp'))
- grad_qkv: float32 [768, 2304], P('dp')
- grad_out_attn: float32 [768, 768], P('dp')
- grad_in_ff: float32 [768, 6144], P('dp')
- grad_out_ff: float32 [3072, 768], P('dp')
- grad_gain_one: float32 [768], replicated
- grad_shift_one: float32 [768], replicated
- grad_gain_two: float32 [768], replicated
- grad_shift_two: float32 [768], replicated
Inputs may be any that keep to these rules, and one draw needn't show every extreme that they name: `masked_rows`: within each device's block of 76 entries the rows are distinct and increasing.
All inputs are finite; a program needn't handle non-finite values.
Results may differ from a plain program's by a relative error of at most 0.017.
Values may be sent and summed in bfloat16 or wider, within the bound.
No kernel may reach another device: no remote copies, remote signals or barrier semaphores. Data moves between devices by JAX's collectives and lax.ppermute only.
A program may use at most 128 MiB of HBM per device.

v0:
```python
import math
import jax
import jax.numpy as jnp
from jax import lax
from jax.sharding import PartitionSpec as P

HEADS = 12
norm_epsilon = 1e-05
masked_score = -1e30


def alibi_slopes(head_count):
    nearest = 2 ** int(math.floor(math.log2(head_count)))
    base_list = [2.0 ** (-8.0 * (index + 1) / nearest) for index in range(nearest)]
    extra_list = [
        2.0 ** (-8.0 * (2 * index + 1) / (2 * nearest)) for index in range(head_count - nearest)
    ]
    return jnp.array(base_list + extra_list, dtype=jnp.float32)


def normalize(value, gain, shift):
    center = value - jnp.mean(value, axis=-1, keepdims=True)
    spread = jnp.mean(center * center, axis=-1, keepdims=True)
    return center * lax.rsqrt(spread + norm_epsilon) * gain + shift


def gated_unit(gate, up_half):
    return jax.nn.gelu(gate, approximate=False) * up_half


def score_block(query_blk, keys, seg_q, seg_k, pos_q, pos_k, slopes, scale):
    raw = jnp.einsum("qhd,khd->hqk", query_blk, keys, preferred_element_type=jnp.float32) * scale
    distance = jnp.abs(pos_q[:, None] - pos_k[None, :]).astype(jnp.float32)
    raw = raw - slopes[:, None, None] * distance[None]
    return jnp.where((seg_q[:, None] == seg_k[None, :])[None], raw, masked_score)


def local(
    tokens,
    segment_ids,
    masked_rows,
    replacement,
    cotangent,
    w_qkv,
    w_out_attn,
    w_in_ff,
    w_out_ff,
    gain_one,
    shift_one,
    gain_two,
    shift_two,
):
    rows_dev, width = tokens.shape
    ranks = lax.axis_size("sp")
    rank = lax.axis_index("sp")
    heads_local = HEADS // ranks
    head_dim = width // HEADS
    local_width = heads_local * head_dim
    hidden_width = w_out_ff.shape[0]
    scale = head_dim ** (-0.5)
    group_seg = segment_ids[0]
    group_tok = group_seg.shape[0]
    block = min(512, group_tok)
    count = group_tok // block
    positions = jnp.arange(group_tok, dtype=jnp.int32)
    slopes = lax.dynamic_slice_in_dim(alibi_slopes(HEADS), rank * heads_local, heads_local, 0)
    select = (jnp.arange(rows_dev, dtype=jnp.int32)[:, None] == masked_rows[None, :]).astype(
        jnp.float32
    )
    placed = jnp.dot(select, replacement.astype(jnp.float32), precision=lax.Precision.HIGHEST)
    hit = jnp.sum(select, axis=1, keepdims=True) > 0.5
    start_low = jnp.where(hit, placed, tokens.astype(jnp.float32)).astype(jnp.bfloat16)
    start = start_low.astype(jnp.float32)
    qkv = jnp.dot(start_low, w_qkv, preferred_element_type=jnp.float32).astype(jnp.bfloat16)
    qkv_heads = lax.all_to_all(
        qkv.reshape(rows_dev, 3, ranks, local_width), "sp", split_axis=2, concat_axis=0, tiled=True
    )
    qkv_heads = qkv_heads.reshape(group_tok, 3, heads_local, head_dim)
    query = qkv_heads[:, 0]
    keys = qkv_heads[:, 1]
    values = qkv_heads[:, 2]

    def forward_block(index):
        first = index * block
        query_blk = lax.dynamic_slice_in_dim(query, first, block, 0)
        seg_q = lax.dynamic_slice_in_dim(group_seg, first, block, 0)
        pos_q = lax.dynamic_slice_in_dim(positions, first, block, 0)
        scores = score_block(query_blk, keys, seg_q, group_seg, pos_q, positions, slopes, scale)
        peak = jnp.max(scores, axis=-1, keepdims=True)
        weights = jnp.exp(scores - peak)
        total = jnp.sum(weights, axis=-1, keepdims=True)
        probs = (weights / total).astype(jnp.bfloat16)
        out = jnp.einsum("hqk,khd->qhd", probs, values, preferred_element_type=jnp.float32)
        return (out.astype(jnp.bfloat16), (peak + jnp.log(total))[..., 0])

    attn_heads, logsum = lax.map(forward_block, jnp.arange(count, dtype=jnp.int32))
    attn_heads = attn_heads.reshape(group_tok, 1, local_width)
    attn_low = lax.all_to_all(attn_heads, "sp", split_axis=0, concat_axis=1, tiled=True).reshape(
        rows_dev, width
    )
    proj = jnp.dot(attn_low, w_out_attn, preferred_element_type=jnp.float32)
    first_norm, pull_one = jax.vjp(normalize, start + proj, gain_one, shift_one)
    first_low = first_norm.astype(jnp.bfloat16)
    mixed = jnp.dot(first_low, w_in_ff, preferred_element_type=jnp.float32)
    hidden, pull_gate = jax.vjp(gated_unit, mixed[:, :hidden_width], mixed[:, hidden_width:])
    hidden_low = hidden.astype(jnp.bfloat16)
    branch = jnp.dot(hidden_low, w_out_ff, preferred_element_type=jnp.float32)
    result, pull_two = jax.vjp(normalize, first_norm + branch, gain_two, shift_two)
    layer_out = result.astype(jnp.bfloat16)
    grad_result = jnp.dot(select, cotangent, precision=lax.Precision.HIGHEST)
    d_second, d_gain_two, d_shift_two = pull_two(grad_result)
    d_branch = d_second.astype(jnp.bfloat16)
    g_out_ff = jnp.einsum("tf,td->fd", hidden_low, d_branch, preferred_element_type=jnp.float32)
    d_hidden = jnp.einsum("td,fd->tf", d_branch, w_out_ff, preferred_element_type=jnp.float32)
    d_gate, d_up = pull_gate(d_hidden)
    d_mixed = jnp.concatenate([d_gate, d_up], axis=1).astype(jnp.bfloat16)
    g_in_ff = jnp.einsum("td,tf->df", first_low, d_mixed, preferred_element_type=jnp.float32)
    d_first = d_second + jnp.einsum(
        "tf,df->td", d_mixed, w_in_ff, preferred_element_type=jnp.float32
    )
    d_sum_one, d_gain_one, d_shift_one = pull_one(d_first)
    d_proj = d_sum_one.astype(jnp.bfloat16)
    g_out_attn = jnp.einsum("tc,td->cd", attn_low, d_proj, preferred_element_type=jnp.float32)
    d_attn = jnp.einsum("td,cd->tc", d_proj, w_out_attn, preferred_element_type=jnp.float32).astype(
        jnp.bfloat16
    )
    d_attn_heads = lax.all_to_all(
        d_attn.reshape(rows_dev, ranks, local_width), "sp", split_axis=1, concat_axis=0, tiled=True
    )
    d_attn_heads = d_attn_heads.reshape(group_tok, heads_local, head_dim)

    def backward_block(carry, index):
        d_keys, d_values = carry
        first = index * block
        query_blk = lax.dynamic_slice_in_dim(query, first, block, 0)
        dout_blk = lax.dynamic_slice_in_dim(d_attn_heads, first, block, 0)
        seg_q = lax.dynamic_slice_in_dim(group_seg, first, block, 0)
        pos_q = lax.dynamic_slice_in_dim(positions, first, block, 0)
        scores = score_block(query_blk, keys, seg_q, group_seg, pos_q, positions, slopes, scale)
        probs = jnp.exp(scores - logsum[index][:, :, None])
        d_probs = jnp.einsum("qhd,khd->hqk", dout_blk, values, preferred_element_type=jnp.float32)
        delta = jnp.sum(probs * d_probs, axis=-1, keepdims=True)
        d_scores = (probs * (d_probs - delta)).astype(jnp.bfloat16)
        d_query = (
            jnp.einsum("hqk,khd->qhd", d_scores, keys, preferred_element_type=jnp.float32) * scale
        )
        d_keys = (
            d_keys
            + jnp.einsum("hqk,qhd->khd", d_scores, query_blk, preferred_element_type=jnp.float32)
            * scale
        )
        d_values = d_values + jnp.einsum(
            "hqk,qhd->khd", probs.astype(jnp.bfloat16), dout_blk, preferred_element_type=jnp.float32
        )
        return ((d_keys, d_values), d_query)

    empty = jnp.zeros((group_tok, heads_local, head_dim), jnp.float32)
    (d_keys, d_values), d_query = lax.scan(
        backward_block, (empty, empty), jnp.arange(count, dtype=jnp.int32)
    )
    d_query = d_query.reshape(group_tok, heads_local, head_dim)
    d_qkv_heads = jnp.stack([d_query, d_keys, d_values], axis=1).astype(jnp.bfloat16)
    d_qkv = lax.all_to_all(
        d_qkv_heads.reshape(group_tok, 3, 1, local_width),
        "sp",
        split_axis=0,
        concat_axis=2,
        tiled=True,
    )
    d_qkv = d_qkv.reshape(rows_dev, 3 * width)
    g_qkv = jnp.einsum("tc,tq->cq", start_low, d_qkv, preferred_element_type=jnp.float32)
    d_start = d_sum_one + jnp.einsum("tq,cq->tc", d_qkv, w_qkv, preferred_element_type=jnp.float32)
    grad_tokens = jnp.where(hit, 0.0, d_start)
    grad_replacement = jnp.einsum("tm,tc->mc", select, d_start, precision=lax.Precision.HIGHEST)
    row_shares = (
        lax.psum_scatter(g_qkv, "dp", scatter_dimension=0, tiled=True),
        lax.psum_scatter(g_out_attn, "dp", scatter_dimension=0, tiled=True),
        lax.psum_scatter(g_in_ff, "dp", scatter_dimension=0, tiled=True),
        lax.psum_scatter(g_out_ff, "dp", scatter_dimension=0, tiled=True),
    )
    share_parts = (
        lax.psum_scatter(
            row_shares[0].astype(jnp.bfloat16), "sp", scatter_dimension=1, tiled=True
        ).astype(jnp.float32),
        lax.psum_scatter(
            row_shares[1].astype(jnp.bfloat16), "sp", scatter_dimension=1, tiled=True
        ).astype(jnp.float32),
        lax.psum_scatter(
            row_shares[2].astype(jnp.bfloat16), "sp", scatter_dimension=1, tiled=True
        ).astype(jnp.float32),
        lax.psum_scatter(
            row_shares[3].astype(jnp.bfloat16), "sp", scatter_dimension=1, tiled=True
        ).astype(jnp.float32),
    )
    summed = (
        lax.all_gather(share_parts[0].astype(jnp.bfloat16), "sp", axis=1, tiled=True).astype(
            jnp.float32
        ),
        lax.all_gather(share_parts[1].astype(jnp.bfloat16), "sp", axis=1, tiled=True).astype(
            jnp.float32
        ),
        lax.all_gather(share_parts[2].astype(jnp.bfloat16), "sp", axis=1, tiled=True).astype(
            jnp.float32
        ),
        lax.all_gather(share_parts[3].astype(jnp.bfloat16), "sp", axis=1, tiled=True).astype(
            jnp.float32
        ),
    )
    norm_sums = lax.psum((d_gain_one, d_shift_one, d_gain_two, d_shift_two), ("dp", "sp"))
    return (
        layer_out,
        grad_tokens,
        grad_replacement,
        summed[0],
        summed[1],
        summed[2],
        summed[3],
        norm_sums[0],
        norm_sums[1],
        norm_sums[2],
        norm_sums[3],
    )


def solution(mesh):
    return jax.shard_map(
        local,
        mesh=mesh,
        in_specs=(
            P(("dp", "sp"), None),
            P("dp", None),
            P(("dp", "sp")),
            P(("dp", "sp"), None),
            P(("dp", "sp"), None),
            P(),
            P(),
            P(),
            P(),
            P(),
            P(),
            P(),
            P(),
        ),
        out_specs=(
            P(("dp", "sp"), None),
            P(("dp", "sp"), None),
            P(("dp", "sp"), None),
            P("dp", None),
            P("dp", None),
            P("dp", None),
            P("dp", None),
            P(),
            P(),
            P(),
            P(),
        ),
        check_vma=False,
    )
```

profile of v0, /device:TPU:0, one launch (start us, length us, event | category | flops | bytes accessed | tf_op | source)
XLA Modules:
  0.0 950.8 jit_solution(5852370499418419649)
XLA Ops:
  13.0 2.4 copy.95
  15.4 2.4 copy.96
  17.7 4.3 all-to-all-start
  22.2 16.4 %all-to-all-done = bf16[256,3,4,192]{0,3,1,2:T(8,128)(2,1)} async-done(((bf16[256,3,4,192]{0,3,1,2:T(8,128)(2,1)}), bf16[256,3,4,192]{0,3,1,2:T(8,128)(2,1)}, u32[]{:S(2)}, u32[]{:S(2)}) %all-to-all-start) | async-done | bytes 1179680 | tf_op jit(solution)/shard_map/all_to_all | solution.py:75
  38.6 3.2 copy.97
  41.8 3.4 reshape.309
  45.2 2.3 slice_bitcast_fusion
  47.5 22.4 %while.29 = (s32[]{:T(128)}, bf16[2,512,3,64]{1,3,2,0:T(8,128)(2,1)}, f32[2,3,512]{2,1,0:T(4,128)}, s32[2]{0:T(128)S(1)}, s32[1024]{0:T(1024)S(1)}, /*index=5*/s...) while((s32[]{:T(128)}, ...), condition=%wide.region_4.5_spmd.clone, body=%wide.region_1.4_spmd.clone.sunk | while | flops 433158656 | bytes 32185620 | solution.py:96
  49.7 3.0 fusion.111
  52.7 2.2 fusion.112
  55.5 3.2 fusion.113
  60.9 3.0 fusion.111
  63.9 2.2 fusion.112
  66.7 3.2 fusion.113
  69.9 2.1 copy.98
  74.5 2.6 reduce
  79.1 2.4 reshape.324
  81.5 11.8 %all_to_all.60 = bf16[4,2,24576]{2,1,0:T(2,128)(2,1)} all-to-all(bf16[4,2,24576]{2,1,0:T(2,128)(2,1)} %reshape.324), channel_id=1, replica_groups=mesh['dp'=8,'sp'=4] {'sp'}, dimensions={0} | all-to-all | bytes 786432 | tf_op jit(solution)/shard_map/all_to_all | solution.py:98
  93.3 3.6 reshape.325
  96.9 3.5 copy.100
  106.4 5.4 fusion.57
  111.7 6.9 multiply_convert_fusion.2
  123.0 4.0 add_convert_fusion
  128.7 8.0 fusion.39
  137.4 8.6 multiply_reduce_fusion.2
  150.5 4.1 all-to-all-start.2
  154.6 3.2 fusion.55
  157.9 4.2 all-to-all-done.2
  166.7 67.6 %while.30 = (s32[]{:T(128)}, f32[1024,3,64]{0,2,1:T(8,128)}, f32[1024,3,64]{0,2,1:T(8,128)}, bf16[2,512,3,64]{1,3,2,0:T(8,128)(2,1)}, s32[2]{0:T(128)}, /*index=...) while((s32[]{:T(128)}, f32[1024,3,64]{0,2,1:T(8,128)}, ...), condition=%wide.region_15.16_spmd.clone.clone, body=%wide.region_13.15_spmd.clone.clone.sunk | while | flops 1027111424 | bytes 128764864 | solution.py:158
  168.7 4.8 fusion.123
  179.2 6.9 multiply_reduce_fusion.8
  186.0 2.6 copy-done.1
  188.6 2.3 multiply_convert_fusion.4
  191.0 3.7 fusion.124
  194.7 3.8 fusion.126
  201.9 4.8 fusion.123
  212.3 6.7 multiply_reduce_fusion.8
  219.0 2.6 copy-done.1
  221.6 2.3 multiply_convert_fusion.4
  223.9 3.9 fusion.124
  227.8 3.7 fusion.126
  231.5 2.7 fusion.125
  234.2 2.1 copy.104
  243.0 4.1 copy.105
  247.0 30.1 %all_to_all.61 = bf16[1024,3,1,192]{3,1,2,0:T(4,128)(2,1)} all-to-all(bf16[1024,3,1,192]{3,1,2,0:T(4,128)(2,1)} %copy.105), channel_id=1, replica_groups=mesh['dp'=8,'sp'=4] {'sp'}, dimensions={0} | all-to-all | bytes 2359296 | tf_op jit(solution)/shard_map/all_to_all | solution.py:163
  277.2 4.3 copy.113
  283.9 5.0 fusion.64
  289.6 6.9 fusion.53
  296.5 154.8 %reduce-scatter.19.cloned.1.call-done = f32[96,6144]{1,0:T(8,128)} async-done(((f32[768,6144]{1,0:T(8,128)}), f32[96,6144]{1,0:T(8,128)}) %reduce-scatter.19.cloned.1.call-update) | async-done | bytes 2359312 | tf_op jit(solution)/shard_map/reduce_scatter | solution.py:178
  451.3 2.8 convert_element_type.119
  454.2 69.2 %reduce-scatter.17.cloned.1.call-done = f32[96,768]{1,0:T(8,128)} async-done(((f32[768,768]{1,0:T(8,128)}), f32[96,768]{1,0:T(8,128)}) %reduce-scatter.17.cloned.1.call-update) | async-done | bytes 294928 | tf_op jit(solution)/shard_map/reduce_scatter | solution.py:177
  526.8 128.3 %reduce-scatter.15.cloned.1.call-done = f32[96,2304]{1,0:T(8,128)} async-done(((f32[768,2304]{1,0:T(8,128)}), f32[96,2304]{1,0:T(8,128)}) %reduce-scatter.15.cloned.1.call-update) | async-done | bytes 884752 | tf_op jit(solution)/shard_map/reduce_scatter | solution.py:176
  659.6 161.9 %reduce-scatter.23.cloned.1.call-done = f32[384,768]{1,0:T(8,128)} async-done(((f32[3072,768]{1,0:T(8,128)}), f32[384,768]{1,0:T(8,128)}) %reduce-scatter.23.cloned.1.call-update) | async-done | bytes 1179664 | tf_op jit(solution)/shard_map/reduce_scatter | solution.py:179
  825.8 23.2 %reduce-scatter.21.cloned.1.call-done = bf16[96,1536]{1,0:T(8,128)(2,1)} async-done(((bf16[96,6144]{1,0:T(8,128)(2,1)}), bf16[96,1536]{1,0:T(8,128)(2,1)}) %reduce-scatter.21.cloned.1.call-update) | async-done | bytes 294928 | tf_op jit(solution)/shard_map/reduce_scatter | solution.py:188
  849.0 39.8 %all-reduce = (f32[768]{0:T(1024)}, f32[768]{0:T(1024)}, f32[768]{0:T(1024)}, f32[768]{0:T(1024)}) all-reduce(f32[768]{0:T(1024)} %get-tuple-element.303, f32[768]{0:T(1024)} %get-tuple-element.306, f32[768]{0:T(1024)S(1)} %copy-done.25, f32[768]{0:T(1024)S(1)} %copy-done.26), channel_id=1, replica_groups=mesh['dp'=8,'sp'=4] {'dp','sp'}, use_global_device_ids=true, to_apply=%region_25.26 | all-reduce | flops 3072 | bytes 24576 | tf_op jit(solution)/shard_map/psum | solution.py:209
  888.8 3.5 broadcast_select_fusion
  893.5 8.6 all_gather.13
  905.5 7.3 all-gather
  914.0 2.7 reshape.317
  916.7 5.2 reduce-scatter.29.cloned.1.call-done
  921.9 8.1 all_gather.15
  930.0 2.3 copy.112
  932.3 8.7 all-gather.3.cloned.1.call-done
  941.0 2.9 convert_element_type.120
  (193 shorter events, 75.4 us)
Async XLA Ops:
  7.2 3.7 copy-start
  8.1 0.6 copy-start.27
  10.1 0.7 copy-start.11
  13.0 9.1 copy-start.36
  17.7 20.8 %all-to-all-start = ((bf16[256,3,4,192]{0,3,1,2:T(8,128)(2,1)}), bf16[256,3,4,192]{0,3,1,2:T(8,128)(2,1)}, u32[]{:S(2)}, u32[]{:S(2)}) async-start(bf16[256,3,4,192]{0,3,1,2:T(8,128)(2,1)} %copy.96), calls=%async_computation | async-start | bytes 2359296 | tf_op jit(solution)/shard_map/all_to_all | solution.py:75
  22.0 429.3 %reduce-scatter.19.cloned.1.call-start = ((), (), s32[]{:S(2)}) async-start(), calls=%async_computation.14 | async-start | bytes 21233664 | tf_op jit(solution)/shard_map/reduce_scatter | solution.py:178
  38.6 8.9 copy-start.16
  52.7 2.8 copy-start.6
  63.9 2.8 copy-start.6
  69.9 23.4 %copy-start.22 = (f32[3]{0:T(128)}, f32[3]{0:T(128)S(1)}, u32[]{:S(2)}) copy-start(f32[3]{0:T(128)S(1)} %get-tuple-element.690) | copy-start | bytes 40
  96.9 9.5 copy-start.17
  96.9 9.5 copy-start.18
  103.4 2.4 copy-start.12
  103.4 15.3 %slice-start.2 = ((s8[4718592]{0:T(1024)(128)(4,1)}), s8[4194304]{0:T(1024)(128)(4,1)S(1)}, s32[]{:S(2)}) async-start(s8[4718592]{0:T(1024)(128)(4,1)} %bitcast.161), calls=%async_computation.23 | async-start | bytes 8388608
  105.5 21.5 %copy-start.3 = (f32[256,768]{1,0:T(8,128)}, f32[256,768]{1,0:T(8,128)S(1)}, u32[]{:S(2)}) copy-start(f32[256,768]{1,0:T(8,128)S(1)} %get-tuple-element.378) | copy-start | bytes 2359300
  105.8 0.5 copy-start.29
  106.3 20.8 %copy-start.20 = (f32[256]{0:T(256)}, f32[256]{0:T(256)S(1)}, u32[]{:S(2)}) copy-start(f32[256]{0:T(256)S(1)} %fusion.49) | copy-start | bytes 3076
  106.3 12.3 %slice-start.3 = ((s8[4718592]{0:T(1024)(128)(4,1)}), s8[524288]{0:T(1024)(128)(4,1)S(1)}, s32[]{:S(2)}) async-start(s8[4718592]{0:T(1024)(128)(4,1)} %bitcast.161), calls=%async_computation.24 | async-start | bytes 1048576
  118.7 1.6 copy-start.9
  118.7 1.8 copy-start.19
  118.7 1.8 copy-start.24
  118.7 1.8 copy-start.31
  118.7 3.2 copy-start.33
  123.0 4.0 copy-start.13
  123.0 4.0 copy-start.34
  127.1 1.2 copy-start.14
  127.1 1.7 copy-start.15
  136.7 0.7 copy-start.21
  137.4 8.6 copy-start.30
  137.4 8.6 copy-start.4
  137.4 9.9 %copy-start.10 = (bf16[768,768]{1,0:T(8,128)(2,1)S(1)}, bf16[768,768]{1,0:T(8,128)(2,1)}, u32[]{:S(2)}) copy-start(bf16[768,768]{1,0:T(8,128)(2,1)} %param.24) | copy-start | bytes 3538948
  146.4 0.9 copy-start.7
  150.5 11.6 %all-to-all-start.2 = ((bf16[256,4,192]{0,2,1:T(8,128)(2,1)}), bf16[256,4,192]{0,2,1:T(8,128)(2,1)}, u32[]{:S(2)}, u32[]{:S(2)}) async-start(bf16[256,4,192]{0,2,1:T(8,128)(2,1)} %bitcast.143), calls=%async_computation.2 | async-start | bytes 786432 | tf_op jit(solution)/shard_map/all_to_all | solution.py:127
  154.6 12.1 %copy-start.23 = (f32[3]{0:T(128)S(1)}, f32[3]{0:T(128)}, u32[]{:S(2)}) copy-start(f32[3]{0:T(128)} %copy-done.22) | copy-start | bytes 40
  154.6 368.8 %reduce-scatter.17.cloned.1.call-start = ((), (), s32[]{:S(2)}) async-start(), calls=%async_computation.13 | async-start | bytes 2654208 | tf_op jit(solution)/shard_map/reduce_scatter | solution.py:177
  157.9 497.3 %reduce-scatter.15.cloned.1.call-start = ((), (), s32[]{:S(2)}) async-start(), calls=%async_computation.12 | async-start | bytes 7962624 | tf_op jit(solution)/shard_map/reduce_scatter | solution.py:176
  179.1 9.5 slice-start
  179.1 9.5 slice-start.1
  186.0 2.6 copy-start.1
  191.0 7.5 copy-start.2
  194.7 3.8 copy-start.5
  212.3 9.3 slice-start
  212.3 9.3 slice-start.1
  219.0 2.6 copy-start.1
  223.9 7.6 copy-start.2
  227.8 3.8 copy-start.5
  282.9 1.0 copy-start.8
  288.9 0.7 copy-start.35
  288.9 532.5 %reduce-scatter.23.cloned.1.call-start = ((), (), s32[]{:S(2)}) async-start(), calls=%async_computation.17 | async-start | bytes 10616832 | tf_op jit(solution)/shard_map/reduce_scatter | solution.py:179
  296.4 552.5 %reduce-scatter.21.cloned.1.call-start = ((), (), s32[]{:S(2)}) async-start(), calls=%async_computation.15 | async-start | bytes 1474560 | tf_op jit(solution)/shard_map/reduce_scatter | solution.py:188
  454.1 439.3 %reduce-scatter.27.cloned.1.call-start = ((), (), s32[]{:S(2)}) async-start(), calls=%async_computation.19 | async-start | bytes 245760
  526.8 322.2 %copy-start.25 = (f32[768]{0:T(1024)S(1)}, f32[768]{0:T(1024)}, u32[]{:S(2)}) copy-start(f32[768]{0:T(1024)} %get-tuple-element.301) | copy-start | bytes 9220
  526.8 322.2 %copy-start.26 = (f32[768]{0:T(1024)S(1)}, f32[768]{0:T(1024)}, u32[]{:S(2)}) copy-start(f32[768]{0:T(1024)} %get-tuple-element.305) | copy-start | bytes 9220
  526.8 362.0 %copy-start.28 = (pred[256]{0:T(512)(128)(4,1)S(1)}, pred[256]{0:T(512)(128)(4,1)}, u32[]{:S(2)}) copy-start(pred[256]{0:T(512)(128)(4,1)} %copy-done.27) | copy-start | bytes 772
  526.8 377.0 %reduce-scatter.25.cloned.1.call-start = ((), (), s32[]{:S(2)}) async-start(), calls=%async_computation.18 | async-start | bytes 737280
  659.3 262.6 %reduce-scatter.29.cloned.1.call-start = ((), (), s32[]{:S(2)}) async-start(), calls=%async_computation.20 | async-start | bytes 737280
  825.7 115.2 %all-gather.3.cloned.1.call-start = ((), (), s32[]{:S(2)}) async-start(), calls=%async_computation.16 | async-start | bytes 1474560 | tf_op jit(solution)/shard_map/all_gather | solution.py:202
  888.8 3.5 copy-start.32
Sparse Core Ops, SparseCore 0:
  136.8 314.3 reduce-scatter.18
  455.4 67.9 reduce-scatter.16
  527.1 128.0 reduce-scatter.14
  659.1 162.3 reduce-scatter.22
  824.0 24.8 reduce-scatter.20
  851.8 19.7 reduce-scatter.26
  874.6 22.0 reduce-scatter.24
  899.8 22.0 reduce-scatter.28
  923.4 17.4 all-gather.2
where the time goes:
time: 961 us; the launch traced here: 951 us
  waiting for transfers between devices  572 us (60%)
  matrix products  111 us (12%)
  blocking collectives  106 us (11%)
  local copies, waits for them, and re-layouts  86.4 us (9%)
  other arithmetic  45.7 us (5%)
  between operations  14.8 us (2%)
    reduce_scatter x1, waiting for transfers between devices, local(): lax.psum_scatter(g_out_ff, 'dp', scatter_dimension=0, tiled=True)  162 us
    reduce_scatter x1, waiting for transfers between devices, local(): lax.psum_scatter(g_in_ff, 'dp', scatter_dimension=0, tiled=True)  155 us
    reduce_scatter x1, waiting for transfers between devices, local(): lax.psum_scatter(g_qkv, 'dp', scatter_dimension=0, tiled=True)  128 us
    reduce_scatter x1, waiting for transfers between devices, local(): lax.psum_scatter(g_out_attn, 'dp', scatter_dimension=0, tiled=True)  69.2 us
    psum x1, blocking collectives, local(): lax.psum((d_gain_one, d_shift_one, d_gain_two, d_shift_two), ('dp', 'sp'))  39.8 us
    all_to_all x1, blocking collectives, local(): lax.all_to_all(d_qkv_heads.reshape(group_tok, 3, 1, local_width), 'sp', s...  30.1 us
    unnamed x79, local copies, waits for them, and re-layouts  26.3 us
    reduce_scatter x1, waiting for transfers between devices, local(): lax.psum_scatter(row_shares[2].astype(jnp.bfloat16), 'sp', scatter_dimens...  23.2 us
  transfers between devices with their start and end apart: 11, of which 9 were waited for; matrix products, arithmetic and copies ran while one was open for 14% of the time, Pallas kernels for 0%

commit v1 on v0

--- a/solution.py
+++ b/solution.py
@@ -160,13 +160,16 @@
     )
     d_query = d_query.reshape(group_tok, heads_local, head_dim)
     d_qkv_heads = jnp.stack([d_query, d_keys, d_values], axis=1).astype(jnp.bfloat16)
-    d_qkv = lax.all_to_all(
-        d_qkv_heads.reshape(group_tok, 3, 1, local_width),
-        "sp",
-        split_axis=0,
-        concat_axis=2,
-        tiled=True,
-    )
+
+    def figure_deliver(field):
+        return jnp.concatenate(
+            lax.all_to_all(
+                jnp.stack(jnp.split(field, lax.axis_size("sp"), axis=0), axis=0), "sp", 0, 0
+            ),
+            2,
+        )
+
+    d_qkv = figure_deliver(d_qkv_heads.reshape(group_tok, 3, 1, local_width))
     d_qkv = d_qkv.reshape(rows_dev, 3 * width)
     g_qkv = jnp.einsum("tc,tq->cq", start_low, d_qkv, preferred_element_type=jnp.float32)
     d_start = d_sum_one + jnp.einsum("tq,cq->tc", d_qkv, w_qkv, preferred_element_type=jnp.float32)

time: 961 us -> 961 us (level)
  waiting for transfers between devices: 572 us -> 596 us
  blocking collectives: 106 us -> 93.8 us
    reduce_scatter x1, waiting for transfers between devices: 155 us -> 179 us  [local(): lax.psum_scatter(g_in_ff, 'dp', scatter_dimension=0, tiled=True)]
    all_to_all x1, blocking collectives: 30.1 us -> 18.3 us  [figure_deliver(): lax.all_to_all(jnp.stack(jnp.split(field, lax.axis_size('sp'), axis=0), a...]
    unnamed x79 -> x81, local copies, waits for them, and re-layouts: 26.3 us -> 26.4 us
  transfers between devices with their start and end apart: 11 -> 11, of which waited for: 9 -> 9; matrix products, arithmetic and copies ran while one was open for 14% -> 13% of each run, Pallas kernels for 0% -> 0%
where the time goes in v1:
time: 961 us; the launch traced here: 951 us
  waiting for transfers between devices  596 us (62%)
  matrix products  110 us (11%)
  blocking collectives  93.8 us (10%)
  local copies, waits for them, and re-layouts  76.9 us (8%)
  other arithmetic  44.1 us (5%)
  between operations  14.8 us (2%)
    reduce_scatter x1, waiting for transfers between devices, local(): lax.psum_scatter(g_in_ff, 'dp', scatter_dimension=0, tiled=True)  179 us
    reduce_scatter x1, waiting for transfers between devices, local(): lax.psum_scatter(g_out_ff, 'dp', scatter_dimension=0, tiled=True)  162 us
    reduce_scatter x1, waiting for transfers between devices, local(): lax.psum_scatter(g_qkv, 'dp', scatter_dimension=0, tiled=True)  128 us
    reduce_scatter x1, waiting for transfers between devices, local(): lax.psum_scatter(g_out_attn, 'dp', scatter_dimension=0, tiled=True)  69.4 us
    psum x1, blocking collectives, local(): lax.psum((d_gain_one, d_shift_one, d_gain_two, d_shift_two), ('dp', 'sp'))  39.8 us
    unnamed x81, local copies, waits for them, and re-layouts  26.4 us
    reduce_scatter x1, waiting for transfers between devices, local(): lax.psum_scatter(row_shares[2].astype(jnp.bfloat16), 'sp', scatter_dimens...  22.8 us
    dot_general x4, matrix products, score_block(): jnp.einsum('qhd,khd->hqk', query_blk, keys, preferred_element_type=jnp.fl...  19.6 us
  transfers between devices with their start and end apart: 11, of which 9 were waited for; matrix products, arithmetic and copies ran while one was open for 13% of the time, Pallas kernels for 0%

profile of v1, /device:TPU:0, one launch (start us, length us, event | category | flops | bytes accessed | tf_op | source)
XLA Modules:
  0.0 951.2 jit_solution(16681458833604609142)
XLA Ops:
  10.8 2.1 convolution_convert_fusion
  13.0 2.4 copy.65
  15.3 2.4 copy.66
  17.7 4.3 all-to-all-start
  22.1 16.4 %all-to-all-done = bf16[256,3,4,192]{0,3,1,2:T(8,128)(2,1)} async-done(((bf16[256,3,4,192]{0,3,1,2:T(8,128)(2,1)}), bf16[256,3,4,192]{0,3,1,2:T(8,128)(2,1)}, u32[]{:S(2)}, u32[]{:S(2)}) %all-to-all-start) | async-done | bytes 1179680 | tf_op jit(solution)/shard_map/all_to_all | solution.py:75
  38.6 3.2 copy.67
  41.8 3.4 reshape.268
  45.2 2.3 slice_bitcast_fusion
  47.5 22.4 %while.29 = (s32[]{:T(128)}, bf16[2,512,3,64]{1,3,2,0:T(8,128)(2,1)}, f32[2,3,512]{2,1,0:T(4,128)}, s32[2]{0:T(128)S(1)}, s32[1024]{0:T(1024)S(1)}, /*index=5*/s...) while((s32[]{:T(128)}, ...), condition=%wide.region_4.5_spmd.clone, body=%wide.region_1.4_spmd.clone.sunk | while | flops 433158656 | bytes 32185620 | solution.py:96
  49.7 3.0 fusion.112
  52.7 2.2 fusion.113
  55.5 3.2 fusion.114
  60.9 3.0 fusion.112
  63.9 2.2 fusion.113
  66.7 3.2 fusion.114
  69.9 2.1 copy.68
  74.6 2.6 reduce
  79.1 2.4 reshape.283
  81.5 11.8 %all_to_all.50 = bf16[4,2,24576]{2,1,0:T(2,128)(2,1)} all-to-all(bf16[4,2,24576]{2,1,0:T(2,128)(2,1)} %reshape.283), channel_id=1, replica_groups=mesh['dp'=8,'sp'=4] {'sp'}, dimensions={0} | all-to-all | bytes 786432 | tf_op jit(solution)/shard_map/all_to_all | solution.py:98
  93.3 3.6 reshape.284
  96.9 3.5 copy.70
  106.4 5.4 fusion.57
  111.8 6.9 multiply_convert_fusion.2
  123.1 4.0 add_convert_fusion
  128.8 8.1 fusion.39
  137.6 8.6 multiply_reduce_fusion.2
  150.7 4.1 all-to-all-start.2
  154.9 3.2 fusion.55
  158.1 4.2 all-to-all-done.2
  166.9 67.4 %while.30 = (s32[]{:T(128)}, f32[1024,3,64]{0,2,1:T(8,128)}, f32[1024,3,64]{0,2,1:T(8,128)}, bf16[2,512,3,64]{1,3,2,0:T(8,128)(2,1)}, s32[2]{0:T(128)}, /*index=...) while((s32[]{:T(128)}, f32[1024,3,64]{0,2,1:T(8,128)}, ...), condition=%wide.region_15.16_spmd.clone.clone, body=%wide.region_13.15_spmd.clone.clone.sunk | while | flops 1027111424 | bytes 128764864 | solution.py:158
  168.9 4.8 fusion.124
  179.2 6.9 multiply_reduce_fusion.8
  186.1 2.6 copy-done.1
  188.7 2.3 multiply_convert_fusion.4
  191.1 3.7 fusion.125
  194.8 3.8 fusion.127
  201.9 4.8 fusion.124
  212.3 6.7 multiply_reduce_fusion.8
  219.0 2.6 copy-done.1
  221.6 2.3 multiply_convert_fusion.4
  224.0 3.9 fusion.125
  227.8 3.7 fusion.127
  231.6 2.7 fusion.126
  234.3 2.1 copy.74
  241.4 18.3 %all_to_all.51 = bf16[4,256,3,1,192]{1,4,2,3,0:T(8,128)(2,1)S(1)} all-to-all(bf16[4,256,3,1,192]{1,4,2,3,0:T(8,128)(2,1)S(1)} %pad_maximum_fusion.6), channel_id=1, replica_groups=mesh['dp'=8,'sp'=4] {'sp'}, dimensions={0} | all-to-all | bytes 2359296 | tf_op jit(solution)/shard_map/all_to_all | solution.py:166
  260.8 4.0 fusion.65
  265.5 6.8 fusion.53
  272.4 179.0 %reduce-scatter.19.cloned.1.call-done = f32[96,6144]{1,0:T(8,128)} async-done(((f32[768,6144]{1,0:T(8,128)}), f32[96,6144]{1,0:T(8,128)}) %reduce-scatter.19.cloned.1.call-update) | async-done | bytes 2359312 | tf_op jit(solution)/shard_map/reduce_scatter | solution.py:181
  451.4 2.8 convert_element_type.112
  454.3 69.4 %reduce-scatter.17.cloned.1.call-done = f32[96,768]{1,0:T(8,128)} async-done(((f32[768,768]{1,0:T(8,128)}), f32[96,768]{1,0:T(8,128)}) %reduce-scatter.17.cloned.1.call-update) | async-done | bytes 294928 | tf_op jit(solution)/shard_map/reduce_scatter | solution.py:180
  527.2 128.3 %reduce-scatter.15.cloned.1.call-done = f32[96,2304]{1,0:T(8,128)} async-done(((f32[768,2304]{1,0:T(8,128)}), f32[96,2304]{1,0:T(8,128)}) %reduce-scatter.15.cloned.1.call-update) | async-done | bytes 884752 | tf_op jit(solution)/shard_map/reduce_scatter | solution.py:179
  659.5 162.3 %reduce-scatter.23.cloned.1.call-done = f32[384,768]{1,0:T(8,128)} async-done(((f32[3072,768]{1,0:T(8,128)}), f32[384,768]{1,0:T(8,128)}) %reduce-scatter.23.cloned.1.call-update) | async-done | bytes 1179664 | tf_op jit(solution)/shard_map/reduce_scatter | solution.py:182
  821.9 2.1 convert_element_type.114
  826.5 22.8 %reduce-scatter.21.cloned.1.call-done = bf16[96,1536]{1,0:T(8,128)(2,1)} async-done(((bf16[96,6144]{1,0:T(8,128)(2,1)}), bf16[96,1536]{1,0:T(8,128)(2,1)}) %reduce-scatter.21.cloned.1.call-update) | async-done | bytes 294928 | tf_op jit(solution)/shard_map/reduce_scatter | solution.py:191
  849.3 39.8 %all-reduce = (f32[768]{0:T(1024)}, f32[768]{0:T(1024)}, f32[768]{0:T(1024)}, f32[768]{0:T(1024)}) all-reduce(f32[768]{0:T(1024)} %get-tuple-element.281, f32[768]{0:T(1024)} %get-tuple-element.284, f32[768]{0:T(1024)S(1)} %copy-done.26, f32[768]{0:T(1024)S(1)} %copy-done.27), channel_id=1, replica_groups=mesh['dp'=8,'sp'=4] {'dp','sp'}, use_global_device_ids=true, to_apply=%region_25.26 | all-reduce | flops 3072 | bytes 24576 | tf_op jit(solution)/shard_map/psum | solution.py:212
  889.2 3.5 broadcast_select_fusion
  893.8 8.6 all_gather.13
  905.8 7.3 all-gather
  914.3 2.7 reshape.276
  917.1 5.2 reduce-scatter.29.cloned.1.call-done
  922.3 8.1 all_gather.15
  930.4 2.3 copy.80
  932.7 8.7 all-gather.3.cloned.1.call-done
  941.4 2.9 convert_element_type.113
  (194 shorter events, 68.2 us)
Async XLA Ops:
  7.2 3.7 copy-start
  8.1 0.5 copy-start.28
  10.1 0.7 copy-start.11
  13.0 9.1 copy-start.37
  17.7 20.9 %all-to-all-start = ((bf16[256,3,4,192]{0,3,1,2:T(8,128)(2,1)}), bf16[256,3,4,192]{0,3,1,2:T(8,128)(2,1)}, u32[]{:S(2)}, u32[]{:S(2)}) async-start(bf16[256,3,4,192]{0,3,1,2:T(8,128)(2,1)} %copy.66), calls=%async_computation | async-start | bytes 2359296 | tf_op jit(solution)/shard_map/all_to_all | solution.py:75
  22.0 429.4 %reduce-scatter.19.cloned.1.call-start = ((), (), s32[]{:S(2)}) async-start(), calls=%async_computation.14 | async-start | bytes 21233664 | tf_op jit(solution)/shard_map/reduce_scatter | solution.py:181
  38.6 8.9 copy-start.17
  52.7 2.8 copy-start.6
  63.9 2.8 copy-start.6
  69.9 23.4 %copy-start.23 = (f32[3]{0:T(128)}, f32[3]{0:T(128)S(1)}, u32[]{:S(2)}) copy-start(f32[3]{0:T(128)S(1)} %get-tuple-element.674) | copy-start | bytes 40
  96.9 9.5 %copy-start.18 = (f32[768]{0:T(1024)S(1)}, f32[768]{0:T(1024)}, u32[]{:S(2)}) copy-start(f32[768]{0:T(1024)} %param.27) | copy-start | bytes 9220
  96.9 9.5 %copy-start.19 = (f32[768]{0:T(1024)S(1)}, f32[768]{0:T(1024)}, u32[]{:S(2)}) copy-start(f32[768]{0:T(1024)} %param.28) | copy-start | bytes 9220
  103.4 2.4 copy-start.13
  103.4 15.3 %slice-start.2 = ((s8[4718592]{0:T(1024)(128)(4,1)}), s8[4194304]{0:T(1024)(128)(4,1)S(1)}, s32[]{:S(2)}) async-start(s8[4718592]{0:T(1024)(128)(4,1)} %bitcast.167), calls=%async_computation.23 | async-start | bytes 8388608
  105.6 21.6 %copy-start.3 = (f32[256,768]{1,0:T(8,128)}, f32[256,768]{1,0:T(8,128)S(1)}, u32[]{:S(2)}) copy-start(f32[256,768]{1,0:T(8,128)S(1)} %get-tuple-element.360) | copy-start | bytes 2359300
  105.8 0.6 copy-start.30
  106.4 20.8 %copy-start.21 = (f32[256]{0:T(256)}, f32[256]{0:T(256)S(1)}, u32[]{:S(2)}) copy-start(f32[256]{0:T(256)S(1)} %fusion.49) | copy-start | bytes 3076
  106.4 12.3 %slice-start.3 = ((s8[4718592]{0:T(1024)(128)(4,1)}), s8[524288]{0:T(1024)(128)(4,1)S(1)}, s32[]{:S(2)}) async-start(s8[4718592]{0:T(1024)(128)(4,1)} %bitcast.167), calls=%async_computation.24 | async-start | bytes 1048576
  118.7 1.6 copy-start.9
  118.8 1.8 copy-start.20
  118.8 1.8 copy-start.25
  118.8 1.8 copy-start.32
  118.8 3.2 copy-start.34
  123.1 4.0 copy-start.14
  123.1 4.0 copy-start.35
  127.1 1.2 copy-start.15
  127.1 1.7 copy-start.16
  136.9 0.7 copy-start.22
  137.6 8.6 copy-start.31
  137.6 8.7 copy-start.4
  137.6 9.9 %copy-start.10 = (bf16[768,768]{1,0:T(8,128)(2,1)S(1)}, bf16[768,768]{1,0:T(8,128)(2,1)}, u32[]{:S(2)}) copy-start(bf16[768,768]{1,0:T(8,128)(2,1)} %param.24) | copy-start | bytes 3538948
  146.6 0.9 copy-start.7
  150.7 11.6 %all-to-all-start.2 = ((bf16[256,4,192]{0,2,1:T(8,128)(2,1)}), bf16[256,4,192]{0,2,1:T(8,128)(2,1)}, u32[]{:S(2)}, u32[]{:S(2)}) async-start(bf16[256,4,192]{0,2,1:T(8,128)(2,1)} %bitcast.147), calls=%async_computation.2 | async-start | bytes 786432 | tf_op jit(solution)/shard_map/all_to_all | solution.py:127
  154.8 12.1 %copy-start.24 = (f32[3]{0:T(128)S(1)}, f32[3]{0:T(128)}, u32[]{:S(2)}) copy-start(f32[3]{0:T(128)} %copy-done.23) | copy-start | bytes 40
  154.8 368.9 %reduce-scatter.17.cloned.1.call-start = ((), (), s32[]{:S(2)}) async-start(), calls=%async_computation.13 | async-start | bytes 2654208 | tf_op jit(solution)/shard_map/reduce_scatter | solution.py:180
  158.1 497.3 %reduce-scatter.15.cloned.1.call-start = ((), (), s32[]{:S(2)}) async-start(), calls=%async_computation.12 | async-start | bytes 7962624 | tf_op jit(solution)/shard_map/reduce_scatter | solution.py:179
  179.2 9.5 slice-start
  179.2 9.5 slice-start.1
  186.1 2.6 copy-start.1
  191.1 7.5 copy-start.2
  194.8 3.8 copy-start.5
  212.3 9.3 slice-start
  212.3 9.3 slice-start.1
  219.0 2.6 copy-start.1
  224.0 7.6 copy-start.2
  227.8 3.7 copy-start.5
  241.2 19.6 %copy-start.12 = (bf16[256,768]{1,0:T(8,128)(2,1)S(1)}, bf16[256,768]{1,0:T(8,128)(2,1)}, u32[]{:S(2)}) copy-start(bf16[256,768]{1,0:T(8,128)(2,1)} %copy-done.11) | copy-start | bytes 1179652
  259.8 1.0 copy-start.8
  264.8 0.7 copy-start.36
  264.8 557.0 %reduce-scatter.23.cloned.1.call-start = ((), (), s32[]{:S(2)}) async-start(), calls=%async_computation.17 | async-start | bytes 10616832 | tf_op jit(solution)/shard_map/reduce_scatter | solution.py:182
  272.4 576.9 %reduce-scatter.21.cloned.1.call-start = ((), (), s32[]{:S(2)}) async-start(), calls=%async_computation.15 | async-start | bytes 1474560 | tf_op jit(solution)/shard_map/reduce_scatter | solution.py:191
  454.3 439.6 %reduce-scatter.27.cloned.1.call-start = ((), (), s32[]{:S(2)}) async-start(), calls=%async_computation.19 | async-start | bytes 245760
  527.1 322.2 %copy-start.26 = (f32[768]{0:T(1024)S(1)}, f32[768]{0:T(1024)}, u32[]{:S(2)}) copy-start(f32[768]{0:T(1024)} %get-tuple-element.279) | copy-start | bytes 9220
  527.1 322.2 %copy-start.27 = (f32[768]{0:T(1024)S(1)}, f32[768]{0:T(1024)}, u32[]{:S(2)}) copy-start(f32[768]{0:T(1024)} %get-tuple-element.283) | copy-start | bytes 9220
  527.1 362.1 %copy-start.29 = (pred[256]{0:T(512)(128)(4,1)S(1)}, pred[256]{0:T(512)(128)(4,1)}, u32[]{:S(2)}) copy-start(pred[256]{0:T(512)(128)(4,1)} %copy-done.28) | copy-start | bytes 772
  527.1 377.0 %reduce-scatter.25.cloned.1.call-start = ((), (), s32[]{:S(2)}) async-start(), calls=%async_computation.18 | async-start | bytes 737280
  659.5 262.8 %reduce-scatter.29.cloned.1.call-start = ((), (), s32[]{:S(2)}) async-start(), calls=%async_computation.20 | async-start | bytes 737280
  826.2 115.2 %all-gather.3.cloned.1.call-start = ((), (), s32[]{:S(2)}) async-start(), calls=%async_computation.16 | async-start | bytes 1474560 | tf_op jit(solution)/shard_map/all_gather | solution.py:205
  889.2 3.5 copy-start.33
Sparse Core Ops, SparseCore 0:
  137.0 314.3 reduce-scatter.18
  455.5 68.1 reduce-scatter.16
  527.4 128.0 reduce-scatter.14
  659.3 162.5 reduce-scatter.22
  824.5 24.7 reduce-scatter.20
  852.2 19.7 reduce-scatter.26
  875.0 22.0 reduce-scatter.24
  900.2 22.0 reduce-scatter.28
  923.9 17.4 all-gather.2
